TPU v7x, 256 devices: a whole 4x4x8 slice. The times are simulated.
256 devices in a mesh: grid: 32 (over z, y), var: 8 (over x, core).
Axes of the slice: x: 4, y: 4, z: 8, core: 2. Of those that a mesh axis runs over, the one named last changes fastest.
Arguments:
- data: bfloat16 [8, 1024, 49152], P('var', None, 'grid'), may hold values from -6 to 6
- area: float32 [49152], P('grid'), may hold values from 0.1 to 1
- eofs: bfloat16 [8, 49152, 128], P('var', 'grid'), may hold values from -0.02734375 to 0.02734375
- var_scale: float32 [8], P('var'), may hold values from 0.5 to 2
- recon_map: bfloat16 [8, 1024, 49152], P('var', None, 'grid'), may hold values from -0.1875 to 0.1875
Outputs:
- fields: bfloat16 [8, 1024, 49152], P('var', None, 'grid')
All inputs are finite; a program needn't handle non-finite values.
Results may differ from a plain program's by a relative error of at most 0.0057.
Values may be sent and summed in bfloat16 or wider, within the bound.
No kernel may reach another device: no remote copies, remote signals or barrier semaphores. Data moves between devices by JAX's collectives and lax.ppermute only.
A program may use at most 64 MiB of HBM per device.

v0:
```python
import jax
import jax.numpy as jnp
from jax import lax
from jax.sharding import PartitionSpec as P


def body(data, area, eofs, var_scale, recon_map):
    scaled = (area[:, None] * eofs[0].astype(jnp.float32)).astype(jnp.bfloat16)
    partial_comps = jnp.dot(data[0], scaled, preferred_element_type=jnp.float32)
    comps = lax.psum(partial_comps, "grid")
    joined_local = (var_scale[0] * comps).astype(jnp.bfloat16)
    patterns = recon_map[0]
    rebuilt = jnp.dot(
        lax.all_gather(joined_local, "var", axis=1, tiled=True),
        patterns,
        preferred_element_type=jnp.float32,
    )
    return rebuilt.astype(jnp.bfloat16)[None]


def solution(mesh):
    placed = (
        P("var", None, "grid"),
        P("grid"),
        P("var", "grid", None),
        P("var"),
        P("var", None, "grid"),
    )
    return jax.shard_map(
        body, mesh=mesh, in_specs=placed, out_specs=P("var", None, "grid"), check_vma=False
    )
```

profile of v0, /device:TPU:1, one launch (start us, length us, event | category | flops | bytes accessed | tf_op | source)
XLA Modules:
  0.0 204.4 jit_solution(12069375334948118248)
XLA Ops:
  6.5 0.0 copy-start
  6.5 0.0 all-reduce.2.cloned.1.call-start
  6.5 4.0 %fusion.4 = f32[1024,128]{1,0:T(8,128)} fusion(bf16[1,1024,1536]{2,1,0:T(8,128)(2,1)} %param.5, bf16[1,1536,128]{2,1,0:T(8,128)(2,1)} %param.7, f32[1536]{0:T(1024)} %param.6), kind=kOutput, calls=%fused_computation.5 | convolution fusion | flops 403243008 | bytes 4069376 | tf_op jit(solution)/shard_map/dot_general | solution.py:9
  10.6 0.0 all-reduce.2.cloned.1.call-update
  10.6 0.0 all-gather.2.cloned.1.call-start
  11.3 146.2 %all-reduce.2.cloned.1.call-done = f32[1024,128]{1,0:T(8,128)} async-done(((f32[1024,128]{1,0:T(8,128)}), f32[1024,128]{1,0:T(8,128)}) %all-reduce.2.cloned.1.call-update) | async-done | bytes 524304 | tf_op jit(solution)/shard_map/psum | solution.py:10
  157.5 1.8 multiply_convert_fusion.1
  159.3 0.0 all-gather.2.cloned.1.call-update
  159.3 31.9 %all-gather.2.cloned.1.call-done = bf16[1024,1024]{1,0:T(8,128)(2,1)} async-done(((bf16[1024,128]{1,0:T(8,128)(2,1)}), bf16[1024,1024]{1,0:T(8,128)(2,1)}) %all-gather.2.cloned.1.call-update) | async-done | bytes 2097168 | tf_op jit(solution)/shard_map/all_gather | solution.py:14
  191.2 0.0 copy-done
  191.2 6.3 %fusion = bf16[1,1024,1536]{2,1,0:T(8,128)(2,1)} fusion(bf16[1024,1024]{1,0:T(8,128)(2,1)} %all-gather.2.cloned.1.call-done, bf16[1,1024,1536]{2,1,0:T(8,128)(2,1)S(1)} %copy-done), kind=kOutput, calls=%fused_computation.1 | convolution fusion | flops 3222798336 | bytes 8388608 | tf_op jit(solution)/shard_map/dot_general | solution.py:13
Async XLA Ops:
  6.5 184.7 %copy-start = (bf16[1,1024,1536]{2,1,0:T(8,128)(2,1)S(1)}, bf16[1,1024,1536]{2,1,0:T(8,128)(2,1)}, u32[]{:S(2)}) copy-start(bf16[1,1024,1536]{2,1,0:T(8,128)(2,1)} %param.9) | copy-start | bytes 9437188
  6.5 151.0 %all-reduce.2.cloned.1.call-start = ((), (), s32[]{:S(2)}) async-start(), calls=%async_computation | async-start | bytes 1048576 | tf_op jit(solution)/shard_map/psum | solution.py:10
  10.6 180.6 %all-gather.2.cloned.1.call-start = ((), (), s32[]{:S(2)}) async-start(), calls=%async_computation.1 | async-start | bytes 2359296 | tf_op jit(solution)/shard_map/all_gather | solution.py:14
Sparse Core Ops, SparseCore 0:
  10.8 146.7 all-reduce.1
  159.5 31.6 all-gather.1
where the time goes:
time: 205 us; the launch traced here: 204 us
  waiting for transfers between devices  178 us (87%)
  between operations  14 us (7%)
  matrix products  10.4 us (5%)
    psum x1, waiting for transfers between devices, body(): comps = lax.psum(partial_comps, 'grid')  146 us
    all_gather x1, waiting for transfers between devices, body(): lax.all_gather(joined_local, 'var', axis=1, tiled=True)  31.9 us
    dot_general x1, matrix products, body(): jnp.dot(lax.all_gather(joined_local, 'var', axis=1, tiled=True), patterns...  6.35 us
  transfers between devices with their start and end apart: 2, of which 2 were waited for; matrix products, arithmetic and copies ran while one was open for 0% of the time, Pallas kernels for 0%

commit v1 on v0

--- a/solution.py
+++ b/solution.py
@@ -2,12 +2,14 @@
 import jax.numpy as jnp
 from jax import lax
 from jax.sharding import PartitionSpec as P
+from jax.lax import all_gather
 
 
 def body(data, area, eofs, var_scale, recon_map):
     scaled = (area[:, None] * eofs[0].astype(jnp.float32)).astype(jnp.bfloat16)
     partial_comps = jnp.dot(data[0], scaled, preferred_element_type=jnp.float32)
-    comps = lax.psum(partial_comps, "grid")
+    moved = all_gather(partial_comps, axis_name="grid")
+    comps = jnp.sum(moved, 0)
     joined_local = (var_scale[0] * comps).astype(jnp.bfloat16)
     patterns = recon_map[0]
     rebuilt = jnp.dot(

time: 205 us -> 224 us (1.093)
  local copies, waits for them, and re-layouts: 0.01 us -> 17.7 us
  other arithmetic: 1.77 us -> 11.6 us
  waiting for transfers between devices: 178 us -> 169 us
    psum x1 -> x0, waiting for transfers between devices: 146 us -> none  [body(): comps = lax.psum(partial_comps, 'grid')]
    all_gather x0 -> x1, waiting for transfers between devices: none -> 143 us  [body(): moved = all_gather(partial_comps, axis_name='grid')]
    unnamed x2 -> x3, local copies, waits for them, and re-layouts: 0.01 us -> 17.7 us
    reduce_sum x0 -> x1, other arithmetic: none -> 9.79 us  [body(): comps = jnp.sum(moved, 0)]
    all_gather x1, waiting for transfers between devices: 31.9 us -> 25.7 us  [body(): lax.all_gather(joined_local, 'var', axis=1, tiled=True)]
where the time goes in v1:
time: 224 us; the launch traced here: 223 us
  waiting for transfers between devices  169 us (75%)
  local copies, waits for them, and re-layouts  17.7 us (8%)
  between operations  14.1 us (6%)
  other arithmetic  11.6 us (5%)
  matrix products  11 us (5%)
    all_gather x1, waiting for transfers between devices, body(): moved = all_gather(partial_comps, axis_name='grid')  143 us
    all_gather x1, waiting for transfers between devices, body(): lax.all_gather(joined_local, 'var', axis=1, tiled=True)  25.7 us
    unnamed x3, local copies, waits for them, and re-layouts  17.7 us
    reduce_sum x1, other arithmetic, body(): comps = jnp.sum(moved, 0)  9.79 us
    dot_general x1, matrix products, body(): jnp.dot(lax.all_gather(joined_local, 'var', axis=1, tiled=True), patterns...  6.5 us
  transfers between devices with their start and end apart: 2, of which 2 were waited for; matrix products, arithmetic and copies ran while one was open for 0% of the time, Pallas kernels for 0%

profile of v1, /device:TPU:1, one launch (start us, length us, event | category | flops | bytes accessed | tf_op | source)
XLA Modules:
  0.0 223.5 jit_solution(17220732359094920945)
XLA Ops:
  6.5 0.0 copy-start
  6.5 0.0 all-gather.6.cloned.1.call-start
  6.5 4.5 %fusion.4 = f32[1024,128]{0,1:T(8,128)} fusion(bf16[1,1024,1536]{2,1,0:T(8,128)(2,1)} %param.5, bf16[1,1536,128]{2,1,0:T(8,128)(2,1)} %param.7, f32[1536]{0:T(1024)} %param.6), kind=kOutput, calls=%fused_computation.6 | convolution fusion | flops 403243008 | bytes 4069376 | tf_op jit(solution)/shard_map/dot_general | solution.py:10
  11.0 0.0 all-gather.6.cloned.1.call-update
  11.0 0.0 all-gather.4.cloned.1.call-start
  11.7 143.4 %all-gather.6.cloned.1.call-done = f32[32768,128]{0,1:T(8,128)} async-done(((f32[1024,128]{0,1:T(8,128)}), f32[32768,128]{0,1:T(8,128)}) %all-gather.6.cloned.1.call-update) | async-done | bytes 16777232 | tf_op jit(solution)/shard_map/all_gather | solution.py:11
  155.2 17.7 %copy.6 = f32[16,8,32,1024]{3,2,1,0:T(8,128)} copy(f32[16,8,32,1024]{3,1,2,0:T(8,128)} %bitcast.23) | data formatting | bytes 33554432
  172.8 9.8 %bitcast_reduce_fusion = f32[1024,128]{0,1:T(8,128)} fusion(f32[16,8,32,1024]{3,2,1,0:T(8,128)} %copy.6), kind=kLoop, calls=%fused_computation | loop fusion | flops 4063232 | bytes 17301504 | tf_op jit(solution)/shard_map/reduce_sum | solution.py:12
  182.6 1.8 multiply_convert_fusion.1
  184.4 0.0 all-gather.4.cloned.1.call-update
  184.4 25.7 %all-gather.4.cloned.1.call-done = bf16[1024,1024]{0,1:T(8,128)(2,1)} async-done(((bf16[1024,128]{0,1:T(8,128)(2,1)}), bf16[1024,1024]{0,1:T(8,128)(2,1)}) %all-gather.4.cloned.1.call-update) | async-done | bytes 2097168 | tf_op jit(solution)/shard_map/all_gather | solution.py:16
  210.1 0.0 copy-done
  210.1 6.5 %fusion = bf16[1,1024,1536]{2,1,0:T(8,128)(2,1)} fusion(bf16[1024,1024]{0,1:T(8,128)(2,1)} %all-gather.4.cloned.1.call-done, bf16[1,1024,1536]{2,1,0:T(8,128)(2,1)S(1)} %copy-done), kind=kOutput, calls=%fused_computation.2 | convolution fusion | flops 3222798336 | bytes 8388608 | tf_op jit(solution)/shard_map/dot_general | solution.py:15
Async XLA Ops:
  6.5 203.6 %copy-start = (bf16[1,1024,1536]{2,1,0:T(8,128)(2,1)S(1)}, bf16[1,1024,1536]{2,1,0:T(8,128)(2,1)}, u32[]{:S(2)}) copy-start(bf16[1,1024,1536]{2,1,0:T(8,128)(2,1)} %param.9) | copy-start | bytes 9437188
  6.5 148.6 %all-gather.6.cloned.1.call-start = ((), (), s32[]{:S(2)}) async-start(), calls=%async_computation.1 | async-start | bytes 17301504 | tf_op jit(solution)/shard_map/all_gather | solution.py:11
  11.0 199.1 %all-gather.4.cloned.1.call-start = ((), (), s32[]{:S(2)}) async-start(), calls=%async_computation | async-start | bytes 2359296 | tf_op jit(solution)/shard_map/all_gather | solution.py:16
Sparse Core Ops, SparseCore 0:
  11.2 143.9 all-gather.5
  184.6 25.5 all-gather.3
